TPU v7x, 32 devices: a whole 2x2x4 slice. The times are simulated.
32 devices in a mesh: space: 8 (over z, y), scene: 4 (over x, core).
Axes of the slice: x: 2, y: 2, z: 4, core: 2. Of those that a mesh axis runs over, the one named last changes fastest.
Arguments:
- features: bfloat16 [4, 16, 64, 512], P('scene', 'space'), may hold values from -6 to 6
- cotangent: bfloat16 [4, 16, 64, 512], P('scene', 'space'), may hold values from -6 to 6
- weight: bfloat16 [27, 64, 64], replicated, may hold values from -0.15625 to 0.15625
- neighbours: int32 [4, 16, 27], P('scene', 'space'), may hold values from -1 to 15, as said below
- occupancy: int32 [4, 16, 512], P('scene', 'space'), may hold values 0 or 1
Outputs:
- conv_out: bfloat16 [4, 16, 64, 512], P('scene', 'space')
- grad_features: bfloat16 [4, 16, 64, 512], P('scene', 'space')
- grad_weight: float32 [27, 64, 64], replicated
Inputs may be any that keep to these rules, and one draw needn't show every extreme that they name: neighbours[s, b, 9 (a + 1) + 3 (c + 1) + (e + 1)] is the number within scene s of the active brick whose brick coordinates differ from brick b's by (a, c, e), each in -1, 0, 1, or -1 where no such brick is active; entry 13 is b itself and the relation is symmetric. Bricks 2 p to 2 (p + 1) - 1 form block p, a slab along the first brick coordinate: a neighbour at offset a = 0 lies in block p, a neighbour in block p - 1 has offset a = -1, a neighbour in block p + 1 has offset a = +1, and no neighbour lies in any other block.
All inputs are finite; a program needn't handle non-finite values. No bound on the sum of `occupancy` on one device may be relied on, other than what follows from the above.
Results may differ from a plain program's by a relative error of at most 0.001.
Values may be sent and summed in bfloat16 or wider, within the bound.
No kernel may reach another device: no remote copies, remote signals or barrier semaphores. Data moves between devices by JAX's collectives and lax.ppermute only.
A program may use at most 64 MiB of HBM per device.

v0:
```python
import math
import jax
import jax.numpy as jnp
from jax import lax
from jax.sharding import PartitionSpec as P


def with_halo(cells, sides, width):
    for axis, dim in sides:
        count = lax.axis_size(axis)
        ends = count - 1
        head = lax.slice_in_dim(cells, 0, width, axis=dim)
        tail = lax.slice_in_dim(cells, cells.shape[dim] - width, cells.shape[dim], axis=dim)
        cells = jnp.concatenate(
            [
                lax.ppermute(tail, axis, [(i, (i + 1) % count) for i in range(ends)]),
                cells,
                lax.ppermute(head, axis, [((i + 1) % count, i) for i in range(ends)]),
            ],
            axis=dim,
        )
    return cells


def bounds(offset):
    if offset == 0:
        return (7, 8)
    if offset == 1:
        return (0, 8)
    return (0, 1)


def assemble(lookup, places):
    plane_list = []
    for off_x in range(3):
        x_low, x_high = bounds(off_x)
        row_list = []
        for off_y in range(3):
            y_low, y_high = bounds(off_y)
            cell_list = []
            for off_z in range(3):
                z_low, z_high = bounds(off_z)
                section = lookup[:, :, x_low:x_high, y_low:y_high, z_low:z_high]
                cell_list.append(
                    jnp.take(section, places[:, 9 * off_x + 3 * off_y + off_z], axis=0)
                )
            row_list.append(jnp.concatenate(cell_list, axis=4))
        plane_list.append(jnp.concatenate(row_list, axis=3))
    return jnp.concatenate(plane_list, axis=2)


def window(volume, start_x, start_y, start_z):
    bricks, channels = (volume.shape[0], volume.shape[1])
    return volume[
        :, :, start_x : start_x + 8, start_y : start_y + 8, start_z : start_z + 8
    ].reshape(bricks, channels, 512)


def local(features, cotangent, weight, neighbours, occupancy):
    bricks, channels = (features.shape[1], features.shape[2])
    grad_scale = 1.0 / math.sqrt(lax.axis_size("scene") * bricks * lax.axis_size("space") * 512)
    present = occupancy[0].astype(jnp.bfloat16)[:, None, :]
    masked_x = features[0] * present
    masked_gradient = cotangent[0] * present
    stacked = jnp.stack([masked_x, masked_gradient])
    gathered = with_halo(stacked, (("space", 1),), bricks)
    zero_rows = jnp.zeros((2, 1, channels, 512), jnp.bfloat16)
    lookup = jnp.concatenate([gathered, zero_rows], axis=1).reshape(
        2, 3 * bricks + 1, channels, 8, 8, 8
    )
    offset_base = (lax.axis_index("space") - 1) * bricks
    places = jnp.where(neighbours[0] < 0, 3 * bricks, neighbours[0] - offset_base)
    volume_x = assemble(lookup[0], places)
    volume_g = assemble(lookup[1], places)
    acc_y = jnp.zeros((bricks, channels, 512), jnp.float32)
    acc_g = jnp.zeros((bricks, channels, 512), jnp.float32)
    partial_w = []
    for tap_x in range(3):
        fwd_list = []
        back_list = []
        back_weights = []
        for inner_tap in range(9):
            tap_y, tap_z = (inner_tap // 3, inner_tap % 3)
            fwd_list.append(window(volume_x, tap_x, tap_y, tap_z))
            back_list.append(window(volume_g, 2 - tap_x, 2 - tap_y, 2 - tap_z))
            back_weights.append(weight[9 * tap_x + inner_tap].T)
        forward_stacked_taps = jnp.concatenate(fwd_list, axis=1)
        backward_stacked_taps = jnp.concatenate(back_list, axis=1)
        forward_kernel_weight = weight[9 * tap_x : 9 * tap_x + 9].reshape(9 * channels, channels)
        backward_kernel_weight = jnp.concatenate(back_weights, axis=0)
        acc_y = acc_y + jnp.einsum(
            "hpo,ps->hso",
            forward_stacked_taps,
            forward_kernel_weight,
            preferred_element_type=jnp.float32,
        )
        acc_g = acc_g + jnp.einsum(
            "ish,sw->iwh",
            backward_stacked_taps,
            backward_kernel_weight,
            preferred_element_type=jnp.float32,
        )
        grouped_weight = jnp.einsum(
            "hgm,htm->gt", forward_stacked_taps, masked_gradient, preferred_element_type=jnp.float32
        )
        partial_w.append(grouped_weight.reshape(9, channels, channels))
    mask_wide = present.astype(jnp.float32)
    out_y = (acc_y * mask_wide).astype(jnp.bfloat16)[None]
    out_g = (acc_g * mask_wide).astype(jnp.bfloat16)[None]
    grad_w = jnp.concatenate(partial_w, axis=0) * grad_scale
    by_scene = lax.psum(grad_w, "scene")
    summed = lax.psum(by_scene, "space")
    return (out_y, out_g, summed)


def solution(mesh):
    in_specs = (
        P("scene", "space", None, None),
        P("scene", "space", None, None),
        P(),
        P("scene", "space", None),
        P("scene", "space", None),
    )
    out_specs = (P("scene", "space", None, None), P("scene", "space", None, None), P())
    return jax.shard_map(local, mesh=mesh, in_specs=in_specs, out_specs=out_specs, check_vma=False)
```

profile of v0, /device:TPU:0, one launch (start us, length us, event | category | flops | bytes accessed | tf_op | source)
XLA Modules:
  0.0 337.7 jit_solution(2646253069375196064)
XLA Ops:
  12.3 5.6 %collective-permute-start = (bf16[2,2,64,512]{2,3,1,0:T(8,128)(2,1)S(1)}, bf16[2,2,64,512]{2,3,1,0:T(8,128)(2,1)S(1)}, u32[]{:S(2)}, u32[]{:S(2)}) collective-permute-start(bf16[2,2,64,512]{2,3,1,0:T(8,128)(2,1)S(1)} %pad_maximum_fusion), channel_id=1, source_target_pairs={{0,4},{4,8},{8,12},{12,16},{16,20},{20,24},{24,28},{1,5},{5,9},{9,... | collective-permute-start | bytes 786440 | tf_op jit(solution)/shard_map/ppermute | solution.py:16
  88.5 1.7 copy.240
  90.2 1.7 copy.241
  91.9 1.7 copy.242
  93.7 1.7 copy.243
  95.4 1.7 copy.244
  97.1 1.7 copy.245
  98.8 1.7 copy.246
  100.6 1.7 copy.247
  103.3 1.8 copy.251
  106.6 1.7 copy.252
  108.3 1.7 copy.253
  113.3 1.8 copy.257
  137.1 1.7 copy.272
  140.4 1.7 copy.273
  142.1 1.7 copy.274
  152.9 1.7 copy.303
  156.2 1.7 copy.304
  157.9 1.7 copy.305
  159.6 1.7 copy.306
  163.1 1.7 copy.308
  164.8 1.7 copy.309
  166.6 1.7 copy.310
  170.0 1.8 copy.314
  173.4 1.7 copy.315
  189.1 1.7 copy.329
  192.4 1.7 copy.330
  205.0 1.8 convolution_bitcast_fusion
  219.7 29.3 %all-reduce.3.cloned.1.call-done = f32[27,64,64]{2,1,0:T(8,128)} async-done(((f32[27,64,64]{2,1,0:T(8,128)}), f32[27,64,64]{2,1,0:T(8,128)}) %all-reduce.3.cloned.1.call-update) | async-done | bytes 442384 | tf_op jit(solution)/shard_map/psum | solution.py:111
  249.9 2.3 fusion.5
  252.2 76.5 %all-reduce.5.cloned.1.call-done = f32[27,64,64]{2,1,0:T(8,128)} async-done(((f32[27,64,64]{2,1,0:T(8,128)}), f32[27,64,64]{2,1,0:T(8,128)}) %all-reduce.5.cloned.1.call-update) | async-done | bytes 442384 | tf_op jit(solution)/shard_map/psum | solution.py:112
  328.7 2.2 copy.476
  (652 shorter events, 158.7 us)
Async XLA Ops:
  7.2 241.8 %all-reduce.3.cloned.1.call-start = ((), (), s32[]{:S(2)}) async-start(), calls=%async_computation | async-start | bytes 1769472 | tf_op jit(solution)/shard_map/psum | solution.py:111
  10.7 16.3 %copy-start.1 = (bf16[27,64,64]{2,1,0:T(8,128)(2,1)S(1)}, bf16[27,64,64]{2,1,0:T(8,128)(2,1)}, u32[]{:S(2)}) copy-start(bf16[27,64,64]{2,1,0:T(8,128)(2,1)} %param.23) | copy-start | bytes 663556
  11.0 32.9 %collective-permute-start.1 = (bf16[2,2,64,512]{2,3,1,0:T(8,128)(2,1)S(1)}, bf16[2,2,64,512]{2,3,1,0:T(8,128)(2,1)S(1)}, u32[]{:S(2)}, u32[]{:S(2)}) collective-permute-start(bf16[2,2,64,512]{2,3,1,0:T(8,128)(2,1)S(1)} %pad_maximum_fusion), channel_id=1, source_target_pairs={{4,0},{8,4},{12,8},{16,12},{20,16},{24,20},{28,24},{5,1},{9,5},{13... | collective-permute-start | bytes 786440 | tf_op jit(solution)/shard_map/ppermute | solution.py:18
  12.3 31.6 %collective-permute-start = (bf16[2,2,64,512]{2,3,1,0:T(8,128)(2,1)S(1)}, bf16[2,2,64,512]{2,3,1,0:T(8,128)(2,1)S(1)}, u32[]{:S(2)}, u32[]{:S(2)}) collective-permute-start(bf16[2,2,64,512]{2,3,1,0:T(8,128)(2,1)S(1)} %pad_maximum_fusion), channel_id=1, source_target_pairs={{0,4},{4,8},{8,12},{12,16},{16,20},{20,24},{24,28},{1,5},{5,9},{9,... | collective-permute-start | bytes 786440 | tf_op jit(solution)/shard_map/ppermute | solution.py:16
  68.7 10.7 %copy-start.132 = (pred[2]{0:T(512)(128)(4,1)S(1)}, pred[2]{0:T(512)(128)(4,1)}, u32[]{:S(2)}) copy-start(pred[2]{0:T(512)(128)(4,1)} %get-tuple-element.275) | copy-start | bytes 10
  68.7 10.7 %copy-start.61 = (bf16[2,64,8]{1,2,0:T(8,128)(2,1)S(1)}, bf16[2,64,8]{1,2,0:T(8,128)(2,1)}, u32[]{:S(2)}) copy-start(bf16[2,64,8]{1,2,0:T(8,128)(2,1)} %gather_fusion.35) | copy-start | bytes 6148
  68.7 10.7 %copy-start.62 = (bf16[2,64,8]{1,2,0:T(8,128)(2,1)S(1)}, bf16[2,64,8]{1,2,0:T(8,128)(2,1)}, u32[]{:S(2)}) copy-start(bf16[2,64,8]{1,2,0:T(8,128)(2,1)} %gather_fusion.17) | copy-start | bytes 6148
  68.7 10.7 %copy-start.157 = (pred[2]{0:T(512)(128)(4,1)S(1)}, pred[2]{0:T(512)(128)(4,1)}, u32[]{:S(2)}) copy-start(pred[2]{0:T(512)(128)(4,1)} %get-tuple-element.245) | copy-start | bytes 10
  69.4 10.7 %copy-start.146 = (pred[2]{0:T(512)(128)(4,1)S(1)}, pred[2]{0:T(512)(128)(4,1)}, u32[]{:S(2)}) copy-start(pred[2]{0:T(512)(128)(4,1)} %get-tuple-element.246) | copy-start | bytes 10
  69.5 10.8 %copy-start.63 = (bf16[2,64,8]{1,2,0:T(8,128)(2,1)S(1)}, bf16[2,64,8]{1,2,0:T(8,128)(2,1)}, u32[]{:S(2)}) copy-start(bf16[2,64,8]{1,2,0:T(8,128)(2,1)} %gather_fusion.33) | copy-start | bytes 6148
  69.5 10.8 %copy-start.64 = (bf16[2,64,8]{1,2,0:T(8,128)(2,1)S(1)}, bf16[2,64,8]{1,2,0:T(8,128)(2,1)}, u32[]{:S(2)}) copy-start(bf16[2,64,8]{1,2,0:T(8,128)(2,1)} %gather_fusion.15) | copy-start | bytes 6148
  69.5 10.8 %copy-start.158 = (pred[2]{0:T(512)(128)(4,1)S(1)}, pred[2]{0:T(512)(128)(4,1)}, u32[]{:S(2)}) copy-start(pred[2]{0:T(512)(128)(4,1)} %get-tuple-element.247) | copy-start | bytes 10
  69.5 11.5 %copy-start.144 = (pred[2]{0:T(512)(128)(4,1)S(1)}, pred[2]{0:T(512)(128)(4,1)}, u32[]{:S(2)}) copy-start(pred[2]{0:T(512)(128)(4,1)} %get-tuple-element.248) | copy-start | bytes 10
  69.5 11.6 %copy-start.143 = (pred[2]{0:T(512)(128)(4,1)S(1)}, pred[2]{0:T(512)(128)(4,1)}, u32[]{:S(2)}) copy-start(pred[2]{0:T(512)(128)(4,1)} %get-tuple-element.249) | copy-start | bytes 10
  115.8 10.2 %copy-start.104 = (bf16[7,64]{1,0:T(8,128)(2,1)S(1)}, bf16[7,64]{1,0:T(8,128)(2,1)}, u32[]{:S(2)}) copy-start(bf16[7,64]{1,0:T(8,128)(2,1)} %get-tuple-element.44) | copy-start | bytes 2692
  115.8 10.8 %copy-start.89 = (bf16[7,64,8]{1,0,2:T(8,128)(2,1)S(1)}, bf16[7,64,8]{1,0,2:T(8,128)(2,1)}, u32[]{:S(2)}) copy-start(bf16[7,64,8]{1,0,2:T(8,128)(2,1)} %get-tuple-element.50) | copy-start | bytes 21508
  115.8 10.8 %copy-start.70 = (bf16[7,64,8]{1,2,0:T(8,128)(2,1)S(1)}, bf16[7,64,8]{1,2,0:T(8,128)(2,1)}, u32[]{:S(2)}) copy-start(bf16[7,64,8]{1,2,0:T(8,128)(2,1)} %get-tuple-element.78) | copy-start | bytes 21508
  115.8 12.9 %copy-start.103 = (bf16[7,64]{1,0:T(8,128)(2,1)S(1)}, bf16[7,64]{1,0:T(8,128)(2,1)}, u32[]{:S(2)}) copy-start(bf16[7,64]{1,0:T(8,128)(2,1)} %get-tuple-element.42) | copy-start | bytes 2692
  115.9 13.6 %copy-start.155 = (pred[2]{0:T(512)(128)(4,1)S(1)}, pred[2]{0:T(512)(128)(4,1)}, u32[]{:S(2)}) copy-start(pred[2]{0:T(512)(128)(4,1)} %get-tuple-element.236) | copy-start | bytes 10
  115.9 14.2 %copy-start.153 = (pred[2]{0:T(512)(128)(4,1)S(1)}, pred[2]{0:T(512)(128)(4,1)}, u32[]{:S(2)}) copy-start(pred[2]{0:T(512)(128)(4,1)} %get-tuple-element.237) | copy-start | bytes 10
  116.7 14.1 %copy-start.154 = (pred[2]{0:T(512)(128)(4,1)S(1)}, pred[2]{0:T(512)(128)(4,1)}, u32[]{:S(2)}) copy-start(pred[2]{0:T(512)(128)(4,1)} %get-tuple-element.238) | copy-start | bytes 10
  116.7 14.7 %copy-start.152 = (pred[2]{0:T(512)(128)(4,1)S(1)}, pred[2]{0:T(512)(128)(4,1)}, u32[]{:S(2)}) copy-start(pred[2]{0:T(512)(128)(4,1)} %get-tuple-element.239) | copy-start | bytes 10
  116.7 15.4 %copy-start.142 = (pred[2]{0:T(512)(128)(4,1)S(1)}, pred[2]{0:T(512)(128)(4,1)}, u32[]{:S(2)}) copy-start(pred[2]{0:T(512)(128)(4,1)} %get-tuple-element.240) | copy-start | bytes 10
  116.7 16.1 %copy-start.151 = (pred[2]{0:T(512)(128)(4,1)S(1)}, pred[2]{0:T(512)(128)(4,1)}, u32[]{:S(2)}) copy-start(pred[2]{0:T(512)(128)(4,1)} %get-tuple-element.241) | copy-start | bytes 10
  117.4 16.0 %copy-start.150 = (pred[2]{0:T(512)(128)(4,1)S(1)}, pred[2]{0:T(512)(128)(4,1)}, u32[]{:S(2)}) copy-start(pred[2]{0:T(512)(128)(4,1)} %get-tuple-element.242) | copy-start | bytes 10
  118.1 16.0 %copy-start.149 = (pred[2]{0:T(512)(128)(4,1)S(1)}, pred[2]{0:T(512)(128)(4,1)}, u32[]{:S(2)}) copy-start(pred[2]{0:T(512)(128)(4,1)} %get-tuple-element.243) | copy-start | bytes 10
  118.1 16.6 %copy-start.148 = (pred[2]{0:T(512)(128)(4,1)S(1)}, pred[2]{0:T(512)(128)(4,1)}, u32[]{:S(2)}) copy-start(pred[2]{0:T(512)(128)(4,1)} %get-tuple-element.244) | copy-start | bytes 10
  118.1 17.2 %copy-start.60 = (bf16[2,64,8,1,8]{1,4,3,2,0:T(8,128)(2,1)S(1)}, bf16[2,64,8,1,8]{1,4,3,2,0:T(8,128)(2,1)}, u32[]{:S(2)}) copy-start(bf16[2,64,8,1,8]{1,4,3,2,0:T(8,128)(2,1)} %copy-done.59) | copy-start | bytes 49156
  118.2 17.2 %copy-start.80 = (bf16[2,64,8,1,1]{1,4,3,2,0:T(2,128)(2,1)S(1)}, bf16[2,64,8,1,1]{1,4,3,2,0:T(2,128)(2,1)}, u32[]{:S(2)}) copy-start(bf16[2,64,8,1,1]{1,4,3,2,0:T(2,128)(2,1)} %copy-done.79) | copy-start | bytes 6148
  118.2 17.2 %copy-start.82 = (bf16[2,64,8,1,1]{1,4,3,2,0:T(2,128)(2,1)S(1)}, bf16[2,64,8,1,1]{1,4,3,2,0:T(2,128)(2,1)}, u32[]{:S(2)}) copy-start(bf16[2,64,8,1,1]{1,4,3,2,0:T(2,128)(2,1)} %copy-done.81) | copy-start | bytes 6148
  211.6 117.1 %all-reduce.5.cloned.1.call-start = ((), (), s32[]{:S(2)}) async-start(), calls=%async_computation.1 | async-start | bytes 1769472 | tf_op jit(solution)/shard_map/psum | solution.py:112
  218.7 30.3 %copy-start.10 = (bf16[9,64,64]{2,1,0:T(8,128)(2,1)S(1)}, bf16[9,64,64]{2,1,0:T(8,128)(2,1)}, u32[]{:S(2)}) copy-start(bf16[9,64,64]{2,1,0:T(8,128)(2,1)} %get-tuple-element.170) | copy-start | bytes 221188
  (135 other events, 584.8 us)
Sparse Core Ops, SparseCore 0:
  211.7 37.2 all-reduce.2
  252.4 76.2 all-reduce.4
where the time goes:
time: 340 us; the launch traced here: 338 us
  local copies, waits for them, and re-layouts  158 us (46%)
  waiting for transfers between devices  106 us (31%)
  other arithmetic  42.7 us (13%)
  between operations  16.4 us (5%)
  matrix products  7.51 us (2%)
  starting transfers between devices  6.93 us (2%)
    psum x1, waiting for transfers between devices, local(): summed = lax.psum(by_scene, 'space')  76.5 us
    reshape x54, local copies, waits for them, and re-layouts, window(): return volume[:, :, start_x:start_x + 8, start_y:start_y + 8, start_z:sta...  67.4 us
    gather x54, local copies, waits for them, and re-layouts, assemble(): jnp.take(section, places[:, 9 * off_x + 3 * off_y + off_z], axis=0)  39.8 us
    psum x1, waiting for transfers between devices, local(): by_scene = lax.psum(grad_w, 'scene')  29.3 us
    unnamed x383, local copies, waits for them, and re-layouts  26.9 us
    gather x23, other arithmetic  13.7 us
    select_n x54, other arithmetic, assemble(): jnp.take(section, places[:, 9 * off_x + 3 * off_y + off_z], axis=0)  11.8 us
    slice x8, local copies, waits for them, and re-layouts, window(): volume[:, :, start_x:start_x + 8, start_y:start_y + 8, start_z:start_z + 8]  8.44 us
  transfers between devices with their start and end apart: 4, of which 2 were waited for; matrix products, arithmetic and copies ran while one was open for 10% of the time, Pallas kernels for 0%

commit v1 on v0

--- a/solution.py
+++ b/solution.py
@@ -3,6 +3,12 @@
 import jax.numpy as jnp
 from jax import lax
 from jax.sharding import PartitionSpec as P
+
+
+def add_all(block, name):
+    parts = lax.all_gather(block, name, axis=0, tiled=False)
+    total = parts.sum(axis=0)
+    return total
 
 
 def with_halo(cells, sides, width):
@@ -108,7 +114,7 @@
     out_y = (acc_y * mask_wide).astype(jnp.bfloat16)[None]
     out_g = (acc_g * mask_wide).astype(jnp.bfloat16)[None]
     grad_w = jnp.concatenate(partial_w, axis=0) * grad_scale
-    by_scene = lax.psum(grad_w, "scene")
+    by_scene = add_all(grad_w, "scene")
     summed = lax.psum(by_scene, "space")
     return (out_y, out_g, summed)
 

time: 340 us -> 333 us (0.979)
  waiting for transfers between devices: 106 us -> 96.2 us
    psum x1 -> x0, waiting for transfers between devices: 29.3 us -> none  [local(): by_scene = lax.psum(grad_w, 'scene')]
    all_gather x0 -> x1, waiting for transfers between devices: none -> 22.6 us  [add_all(): parts = lax.all_gather(block, name, axis=0, tiled=False)]
    reduce_sum x0 -> x1, other arithmetic: none -> 3.43 us  [add_all(): total = parts.sum(axis=0)]
    unnamed x383 -> x391, local copies, waits for them, and re-layouts: 26.9 us -> 25.9 us
  transfers between devices with their start and end apart: 4 -> 4, of which waited for: 2 -> 2; matrix products, arithmetic and copies ran while one was open for 10% -> 11% of each run, Pallas kernels for 0% -> 0%
where the time goes in v1:
time: 333 us; the launch traced here: 331 us
  local copies, waits for them, and re-layouts  158 us (47%)
  waiting for transfers between devices  96.2 us (29%)
  other arithmetic  45.9 us (14%)
  between operations  16.3 us (5%)
  matrix products  7.5 us (2%)
  starting transfers between devices  6.93 us (2%)
    psum x1, waiting for transfers between devices, local(): summed = lax.psum(by_scene, 'space')  73.6 us
    reshape x54, local copies, waits for them, and re-layouts, window(): return volume[:, :, start_x:start_x + 8, start_y:start_y + 8, start_z:sta...  67.7 us
    gather x54, local copies, waits for them, and re-layouts, assemble(): jnp.take(section, places[:, 9 * off_x + 3 * off_y + off_z], axis=0)  39.8 us
    unnamed x391, local copies, waits for them, and re-layouts  25.9 us
    all_gather x1, waiting for transfers between devices, add_all(): parts = lax.all_gather(block, name, axis=0, tiled=False)  22.6 us
    gather x23, other arithmetic  13.7 us
    select_n x54, other arithmetic, assemble(): jnp.take(section, places[:, 9 * off_x + 3 * off_y + off_z], axis=0)  11.9 us
    slice x8, local copies, waits for them, and re-layouts, window(): volume[:, :, start_x:start_x + 8, start_y:start_y + 8, start_z:start_z + 8]  8.47 us
  transfers between devices with their start and end apart: 4, of which 2 were waited for; matrix products, arithmetic and copies ran while one was open for 11% of the time, Pallas kernels for 0%

profile of v1, /device:TPU:0, one launch (start us, length us, event | category | flops | bytes accessed | tf_op | source)
XLA Modules:
  0.0 331.2 jit_solution(5783279187783766611)
XLA Ops:
  12.3 5.6 %collective-permute-start = (bf16[2,2,64,512]{2,3,1,0:T(8,128)(2,1)S(1)}, bf16[2,2,64,512]{2,3,1,0:T(8,128)(2,1)S(1)}, u32[]{:S(2)}, u32[]{:S(2)}) collective-permute-start(bf16[2,2,64,512]{2,3,1,0:T(8,128)(2,1)S(1)} %pad_maximum_fusion), channel_id=1, source_target_pairs={{0,4},{4,8},{8,12},{12,16},{16,20},{20,24},{24,28},{1,5},{5,9},{9,... | collective-permute-start | bytes 786440 | tf_op jit(solution)/shard_map/ppermute | solution.py:22
  88.3 1.7 copy.374
  90.1 1.7 copy.375
  91.8 1.7 copy.376
  93.5 1.7 copy.377
  95.2 1.7 copy.378
  97.0 1.7 copy.379
  98.7 1.7 copy.380
  100.4 1.7 copy.381
  103.1 1.8 copy.385
  106.4 1.7 copy.386
  108.2 1.7 copy.387
  113.1 1.8 copy.391
  137.0 1.7 copy.406
  140.2 1.7 copy.407
  142.0 1.7 copy.408
  152.7 1.7 copy.437
  156.0 1.7 copy.438
  157.7 1.7 copy.439
  159.4 1.7 copy.440
  161.2 1.7 copy.441
  162.9 1.7 copy.442
  164.6 1.7 copy.443
  166.4 1.7 copy.444
  168.1 1.7 copy.445
  190.7 1.7 copy.464
  203.2 1.8 convolution_bitcast_fusion
  219.4 22.6 %all-gather.2.cloned.1.call-done = f32[4,27,64,64]{3,2,1,0:T(8,128)} async-done(((f32[1,27,64,64]{3,2,1,0:T(8,128)}), f32[4,27,64,64]{3,2,1,0:T(8,128)}) %all-gather.2.cloned.1.call-update) | async-done | bytes 1769488 | tf_op jit(solution)/shard_map/all_gather | solution.py:9
  241.9 3.4 %reduce_sum.9 = f32[27,64,64]{2,1,0:T(8,128)} reduce(f32[4,27,64,64]{3,2,1,0:T(8,128)} %all-gather.2.cloned.1.call-done, f32[]{:T(128)} %constant.81.clone.1), dimensions={0}, to_apply=%region_0.9 | reduce | flops 331776 | bytes 2211844 | tf_op jit(solution)/shard_map/reduce_sum | solution.py:10
  246.3 2.3 fusion.5
  248.6 73.6 %all-reduce.2.cloned.1.call-done = f32[27,64,64]{2,1,0:T(8,128)} async-done(((f32[27,64,64]{2,1,0:T(8,128)}), f32[27,64,64]{2,1,0:T(8,128)}) %all-reduce.2.cloned.1.call-update) | async-done | bytes 442384 | tf_op jit(solution)/shard_map/psum | solution.py:118
  322.1 2.2 copy.609
  (661 shorter events, 160.2 us)
Async XLA Ops:
  7.2 234.8 %all-gather.2.cloned.1.call-start = ((), (), s32[]{:S(2)}) async-start(), calls=%async_computation | async-start | bytes 4423680 | tf_op jit(solution)/shard_map/all_gather | solution.py:9
  10.7 16.2 %copy-start.1 = (bf16[27,64,64]{2,1,0:T(8,128)(2,1)S(1)}, bf16[27,64,64]{2,1,0:T(8,128)(2,1)}, u32[]{:S(2)}) copy-start(bf16[27,64,64]{2,1,0:T(8,128)(2,1)} %param.23) | copy-start | bytes 663556
  11.0 32.7 %collective-permute-start.1 = (bf16[2,2,64,512]{2,3,1,0:T(8,128)(2,1)S(1)}, bf16[2,2,64,512]{2,3,1,0:T(8,128)(2,1)S(1)}, u32[]{:S(2)}, u32[]{:S(2)}) collective-permute-start(bf16[2,2,64,512]{2,3,1,0:T(8,128)(2,1)S(1)} %pad_maximum_fusion), channel_id=1, source_target_pairs={{4,0},{8,4},{12,8},{16,12},{20,16},{24,20},{28,24},{5,1},{9,5},{13... | collective-permute-start | bytes 786440 | tf_op jit(solution)/shard_map/ppermute | solution.py:24
  12.3 31.4 %collective-permute-start = (bf16[2,2,64,512]{2,3,1,0:T(8,128)(2,1)S(1)}, bf16[2,2,64,512]{2,3,1,0:T(8,128)(2,1)S(1)}, u32[]{:S(2)}, u32[]{:S(2)}) collective-permute-start(bf16[2,2,64,512]{2,3,1,0:T(8,128)(2,1)S(1)} %pad_maximum_fusion), channel_id=1, source_target_pairs={{0,4},{4,8},{8,12},{12,16},{16,20},{20,24},{24,28},{1,5},{5,9},{9,... | collective-permute-start | bytes 786440 | tf_op jit(solution)/shard_map/ppermute | solution.py:22
  68.6 10.7 %copy-start.136 = (pred[2]{0:T(512)(128)(4,1)S(1)}, pred[2]{0:T(512)(128)(4,1)}, u32[]{:S(2)}) copy-start(pred[2]{0:T(512)(128)(4,1)} %get-tuple-element.275) | copy-start | bytes 10
  68.6 10.7 %copy-start.65 = (bf16[2,64,8]{1,2,0:T(8,128)(2,1)S(1)}, bf16[2,64,8]{1,2,0:T(8,128)(2,1)}, u32[]{:S(2)}) copy-start(bf16[2,64,8]{1,2,0:T(8,128)(2,1)} %gather_fusion.35) | copy-start | bytes 6148
  68.6 10.7 %copy-start.66 = (bf16[2,64,8]{1,2,0:T(8,128)(2,1)S(1)}, bf16[2,64,8]{1,2,0:T(8,128)(2,1)}, u32[]{:S(2)}) copy-start(bf16[2,64,8]{1,2,0:T(8,128)(2,1)} %gather_fusion.17) | copy-start | bytes 6148
  68.6 10.7 %copy-start.161 = (pred[2]{0:T(512)(128)(4,1)S(1)}, pred[2]{0:T(512)(128)(4,1)}, u32[]{:S(2)}) copy-start(pred[2]{0:T(512)(128)(4,1)} %get-tuple-element.245) | copy-start | bytes 10
  69.3 10.7 %copy-start.150 = (pred[2]{0:T(512)(128)(4,1)S(1)}, pred[2]{0:T(512)(128)(4,1)}, u32[]{:S(2)}) copy-start(pred[2]{0:T(512)(128)(4,1)} %get-tuple-element.246) | copy-start | bytes 10
  69.3 10.8 %copy-start.67 = (bf16[2,64,8]{1,2,0:T(8,128)(2,1)S(1)}, bf16[2,64,8]{1,2,0:T(8,128)(2,1)}, u32[]{:S(2)}) copy-start(bf16[2,64,8]{1,2,0:T(8,128)(2,1)} %gather_fusion.33) | copy-start | bytes 6148
  69.4 10.8 %copy-start.68 = (bf16[2,64,8]{1,2,0:T(8,128)(2,1)S(1)}, bf16[2,64,8]{1,2,0:T(8,128)(2,1)}, u32[]{:S(2)}) copy-start(bf16[2,64,8]{1,2,0:T(8,128)(2,1)} %gather_fusion.15) | copy-start | bytes 6148
  69.4 10.8 %copy-start.162 = (pred[2]{0:T(512)(128)(4,1)S(1)}, pred[2]{0:T(512)(128)(4,1)}, u32[]{:S(2)}) copy-start(pred[2]{0:T(512)(128)(4,1)} %get-tuple-element.247) | copy-start | bytes 10
  69.4 11.5 %copy-start.148 = (pred[2]{0:T(512)(128)(4,1)S(1)}, pred[2]{0:T(512)(128)(4,1)}, u32[]{:S(2)}) copy-start(pred[2]{0:T(512)(128)(4,1)} %get-tuple-element.248) | copy-start | bytes 10
  69.4 11.6 %copy-start.147 = (pred[2]{0:T(512)(128)(4,1)S(1)}, pred[2]{0:T(512)(128)(4,1)}, u32[]{:S(2)}) copy-start(pred[2]{0:T(512)(128)(4,1)} %get-tuple-element.249) | copy-start | bytes 10
  115.7 10.1 %copy-start.108 = (bf16[7,64]{1,0:T(8,128)(2,1)S(1)}, bf16[7,64]{1,0:T(8,128)(2,1)}, u32[]{:S(2)}) copy-start(bf16[7,64]{1,0:T(8,128)(2,1)} %get-tuple-element.44) | copy-start | bytes 2692
  115.7 10.8 %copy-start.93 = (bf16[7,64,8]{1,0,2:T(8,128)(2,1)S(1)}, bf16[7,64,8]{1,0,2:T(8,128)(2,1)}, u32[]{:S(2)}) copy-start(bf16[7,64,8]{1,0,2:T(8,128)(2,1)} %get-tuple-element.50) | copy-start | bytes 21508
  115.7 10.8 %copy-start.74 = (bf16[7,64,8]{1,2,0:T(8,128)(2,1)S(1)}, bf16[7,64,8]{1,2,0:T(8,128)(2,1)}, u32[]{:S(2)}) copy-start(bf16[7,64,8]{1,2,0:T(8,128)(2,1)} %get-tuple-element.78) | copy-start | bytes 21508
  115.7 12.9 %copy-start.107 = (bf16[7,64]{1,0:T(8,128)(2,1)S(1)}, bf16[7,64]{1,0:T(8,128)(2,1)}, u32[]{:S(2)}) copy-start(bf16[7,64]{1,0:T(8,128)(2,1)} %get-tuple-element.42) | copy-start | bytes 2692
  115.7 13.6 %copy-start.159 = (pred[2]{0:T(512)(128)(4,1)S(1)}, pred[2]{0:T(512)(128)(4,1)}, u32[]{:S(2)}) copy-start(pred[2]{0:T(512)(128)(4,1)} %get-tuple-element.236) | copy-start | bytes 10
  115.7 14.2 %copy-start.157 = (pred[2]{0:T(512)(128)(4,1)S(1)}, pred[2]{0:T(512)(128)(4,1)}, u32[]{:S(2)}) copy-start(pred[2]{0:T(512)(128)(4,1)} %get-tuple-element.237) | copy-start | bytes 10
  116.5 14.1 %copy-start.158 = (pred[2]{0:T(512)(128)(4,1)S(1)}, pred[2]{0:T(512)(128)(4,1)}, u32[]{:S(2)}) copy-start(pred[2]{0:T(512)(128)(4,1)} %get-tuple-element.238) | copy-start | bytes 10
  116.5 14.8 %copy-start.156 = (pred[2]{0:T(512)(128)(4,1)S(1)}, pred[2]{0:T(512)(128)(4,1)}, u32[]{:S(2)}) copy-start(pred[2]{0:T(512)(128)(4,1)} %get-tuple-element.239) | copy-start | bytes 10
  116.5 15.4 %copy-start.146 = (pred[2]{0:T(512)(128)(4,1)S(1)}, pred[2]{0:T(512)(128)(4,1)}, u32[]{:S(2)}) copy-start(pred[2]{0:T(512)(128)(4,1)} %get-tuple-element.240) | copy-start | bytes 10
  116.5 16.1 %copy-start.155 = (pred[2]{0:T(512)(128)(4,1)S(1)}, pred[2]{0:T(512)(128)(4,1)}, u32[]{:S(2)}) copy-start(pred[2]{0:T(512)(128)(4,1)} %get-tuple-element.241) | copy-start | bytes 10
  117.2 16.1 %copy-start.154 = (pred[2]{0:T(512)(128)(4,1)S(1)}, pred[2]{0:T(512)(128)(4,1)}, u32[]{:S(2)}) copy-start(pred[2]{0:T(512)(128)(4,1)} %get-tuple-element.242) | copy-start | bytes 10
  117.9 16.0 %copy-start.153 = (pred[2]{0:T(512)(128)(4,1)S(1)}, pred[2]{0:T(512)(128)(4,1)}, u32[]{:S(2)}) copy-start(pred[2]{0:T(512)(128)(4,1)} %get-tuple-element.243) | copy-start | bytes 10
  118.0 16.7 %copy-start.152 = (pred[2]{0:T(512)(128)(4,1)S(1)}, pred[2]{0:T(512)(128)(4,1)}, u32[]{:S(2)}) copy-start(pred[2]{0:T(512)(128)(4,1)} %get-tuple-element.244) | copy-start | bytes 10
  118.0 17.3 %copy-start.64 = (bf16[2,64,8,1,8]{1,4,3,2,0:T(8,128)(2,1)S(1)}, bf16[2,64,8,1,8]{1,4,3,2,0:T(8,128)(2,1)}, u32[]{:S(2)}) copy-start(bf16[2,64,8,1,8]{1,4,3,2,0:T(8,128)(2,1)} %copy-done.63) | copy-start | bytes 49156
  118.0 17.3 %copy-start.84 = (bf16[2,64,8,1,1]{1,4,3,2,0:T(2,128)(2,1)S(1)}, bf16[2,64,8,1,1]{1,4,3,2,0:T(2,128)(2,1)}, u32[]{:S(2)}) copy-start(bf16[2,64,8,1,1]{1,4,3,2,0:T(2,128)(2,1)} %copy-done.83) | copy-start | bytes 6148
  118.0 17.3 %copy-start.86 = (bf16[2,64,8,1,1]{1,4,3,2,0:T(2,128)(2,1)S(1)}, bf16[2,64,8,1,1]{1,4,3,2,0:T(2,128)(2,1)}, u32[]{:S(2)}) copy-start(bf16[2,64,8,1,1]{1,4,3,2,0:T(2,128)(2,1)} %copy-done.85) | copy-start | bytes 6148
  209.4 112.7 %all-reduce.2.cloned.1.call-start = ((), (), s32[]{:S(2)}) async-start(), calls=%async_computation.1 | async-start | bytes 1769472 | tf_op jit(solution)/shard_map/psum | solution.py:118
  219.4 26.0 %copy-start.10 = (bf16[9,64,64]{2,1,0:T(8,128)(2,1)S(1)}, bf16[9,64,64]{2,1,0:T(8,128)(2,1)}, u32[]{:S(2)}) copy-start(bf16[9,64,64]{2,1,0:T(8,128)(2,1)} %get-tuple-element.170) | copy-start | bytes 221188
  (139 other events, 606.2 us)
Sparse Core Ops, SparseCore 0:
  209.6 32.3 all-gather.1
  246.0 76.1 all-reduce.1
